TPU v7x, 256 devices: a whole 4x4x8 slice. The times are simulated.
256 devices in a mesh: blk: 32 (over x, z), uly: 8 (over y, core).
Axes of the slice: x: 4, y: 4, z: 8, core: 2. Of those that a mesh axis runs over, the one named last changes fastest.
Arguments:
- tokens: bfloat16 [12288, 3072], P(('blk', 'uly')), may hold values from -6 to 6
- mod_shift: float32 [3072], replicated, may hold values from -3 to 3
- mod_scale: float32 [3072], replicated, may hold values from -2 to 6
- out_gate: float32 [3072], replicated, may hold values from 0.5 to 1.5
- w_qkv: bfloat16 [3072, 24, 384], P(None, 'uly'), may hold values from -0.109375 to 0.109375
- w_out: bfloat16 [3072, 3072], P('uly'), may hold values from -0.109375 to 0.109375
- tile_map: int32 [32], replicated, may hold values from 0 to 31, as said below
- window_corner: int32 [32, 2], replicated, may hold values from 0 to 5, as said below
Outputs:
- mixed: bfloat16 [12288, 3072], P(('blk', 'uly'))
Inputs may be any that keep to these rules, and one draw needn't show every extreme that they name: `tile_map`: A permutation of the tile positions; position j holds a grid tile whose number differs from j by at most 1. `window_corner`: each query tile's 3 x 3 window lies inside the grid and contains the grid tile that its own position holds.
All inputs are finite; a program needn't handle non-finite values.
Results may differ from a plain program's by a relative error of at most 0.02.
The roundings to bfloat16 on the way count: a program that leaves them out, or rounds other values in their place, can miss the bound.
Values may be sent and summed in bfloat16 or wider, within the bound.
A program may use at most 128 MiB of HBM per device.

v0:
```python
import jax
import jax.numpy as jnp
from jax import lax
from jax.sharding import PartitionSpec as P

TILE = 384
WIN = 3
GW = 4


def from_behind(block, axis, distance):
    devices = range(lax.axis_size(axis))
    route = [(i - distance, i) for i in devices if i - distance in devices]
    return lax.ppermute(block, axis, route)


def on_device(tokens, mod_shift, mod_scale, out_gate, w_qkv, w_out, tile_map, window_corner):
    values_in = tokens.astype(jnp.float32)
    mean_row = jnp.mean(values_in, axis=-1, keepdims=True)
    centred = values_in - mean_row
    variance = jnp.mean(centred * centred, axis=-1, keepdims=True)
    normed = (centred * lax.rsqrt(variance + 1e-06) * (1.0 + mod_scale) + mod_shift).astype(
        jnp.bfloat16
    )
    heads_dev = w_qkv.shape[1]
    head_dim = w_qkv.shape[2] // 3
    qkv = jnp.einsum(
        "td,dhe->the",
        lax.all_gather(normed, "uly", axis=0, tiled=True),
        w_qkv,
        preferred_element_type=jnp.float32,
    ).astype(jnp.bfloat16)
    group_rows = qkv.shape[0]
    tiles_here = group_rows // TILE
    all_tiles = tile_map.shape[0]
    queries = qkv[:, :, :head_dim]
    keyval = qkv[:, :, head_dim:]
    shard_idx = lax.axis_index("blk")
    n_blk = lax.axis_size("blk")
    first_tile = shard_idx * tiles_here
    query_corner = lax.dynamic_slice(window_corner, (first_tile, 0), (tiles_here, 2))
    softmax_factor = 1.0 / jnp.sqrt(jnp.float32(head_dim))

    def attend(running, kv_tile, key_tile, is_valid):
        safe_tile = jnp.clip(key_tile, 0, all_tiles - 1)
        key_grid = lax.dynamic_index_in_dim(tile_map, safe_tile, keepdims=False)
        row_gap = key_grid // GW - query_corner[:, 0]
        col_gap = key_grid % GW - query_corner[:, 1]
        inside = (row_gap >= 0) & (row_gap < WIN) & (col_gap >= 0) & (col_gap < WIN) & is_valid

        def compute(state):
            highest, total, accum = state
            row_ok = jnp.repeat(inside, TILE)[None, :, None]
            scores = (
                jnp.einsum(
                    "qhd,khd->hqk",
                    queries,
                    kv_tile[:, :, :head_dim],
                    preferred_element_type=jnp.float32,
                )
                * softmax_factor
            )
            scores = jnp.where(row_ok, scores, -1e30)
            new_high = jnp.maximum(highest, jnp.max(scores, axis=-1))
            probs = jnp.where(row_ok, jnp.exp(scores - new_high[:, :, None]), 0.0)
            factor = jnp.exp(highest - new_high)
            total = total * factor + jnp.sum(probs, axis=-1)
            weights = probs.astype(jnp.bfloat16)
            accum = accum * factor[:, :, None] + jnp.einsum(
                "hqk,khd->hqd",
                weights,
                kv_tile[:, :, head_dim:],
                preferred_element_type=jnp.float32,
            )
            return (new_high, total, accum)

        def keep(state):
            return state

        return lax.cond(jnp.any(inside), compute, keep, running)

    def attend_group(running, arrived, source):
        is_valid = (source >= 0) & (source < n_blk)
        running = attend(running, arrived, source * tiles_here + 0, is_valid)
        return running

    running = (
        jnp.full((heads_dev, group_rows), -1e30, jnp.float32),
        jnp.zeros((heads_dev, group_rows), jnp.float32),
        jnp.zeros((heads_dev, group_rows, head_dim), jnp.float32),
    )
    reach = min((2 * GW + 3 + tiles_here) // tiles_here, n_blk - 1)
    running = attend_group(running, keyval, shard_idx)
    for offset in range(-reach, reach + 1):
        if offset != 0:
            arrived = from_behind(keyval, "blk", offset)
            running = attend_group(running, arrived, shard_idx - offset)
    highest, total, accum = running
    attn = (accum / total[:, :, None]).astype(jnp.bfloat16)
    attn = jnp.transpose(attn, (1, 0, 2)).reshape(group_rows, heads_dev * head_dim)
    summed = lax.psum_scatter(
        jnp.dot(attn, w_out, preferred_element_type=jnp.float32).astype(jnp.bfloat16),
        "uly",
        scatter_dimension=0,
        tiled=True,
    ).astype(jnp.float32)
    return (out_gate * summed).astype(jnp.bfloat16)


def solution(mesh):
    in_specs = (
        P(("blk", "uly"), None),
        P(),
        P(),
        P(),
        P(None, "uly", None),
        P("uly", None),
        P(),
        P(),
    )
    out_specs = P(("blk", "uly"), None)
    return jax.shard_map(
        on_device, mesh=mesh, in_specs=in_specs, out_specs=out_specs, check_vma=False
    )
```

profile of v0, /device:TPU:4, one launch (start us, length us, event | category | flops | bytes accessed | tf_op | source)
XLA Modules:
  0.0 685.6 jit_solution(6186179026058369950)
XLA Ops:
  11.7 31.2 %all-gather.2.cloned.1.call-done = bf16[384,3072]{1,0:T(8,128)(2,1)} async-done(((bf16[48,3072]{1,0:T(8,128)(2,1)}), bf16[384,3072]{1,0:T(8,128)(2,1)}) %all-gather.2.cloned.1.call-update) | async-done | bytes 2359312 | tf_op jit(solution)/shard_map/all_gather | solution.py:29
  42.9 6.9 %fusion.378 = bf16[384,3,384]{2,0,1:T(8,128)(2,1)S(1)} fusion(bf16[3072,3,384]{2,0,1:T(8,128)(2,1)} %param.62, bf16[384,3072]{1,0:T(8,128)(2,1)} %all-gather.2.cloned.1.call-done), kind=kOutput, calls=%fused_computation.479 | convolution fusion | flops 2718351360 | bytes 10321920 | tf_op jit(solution)/shard_map/td,dhe->the/dot_general | solution.py:27
  51.6 7.6 %collective-permute-start = (bf16[384,3,256]{2,0,1:T(8,128)(2,1)}, bf16[384,3,256]{2,0,1:T(8,128)(2,1)}, u32[]{:S(2)}, u32[]{:S(2)}) collective-permute-start(bf16[384,3,256]{2,0,1:T(8,128)(2,1)} %slice.214), channel_id=1, source_target_pairs={{96,0},{104,8},{112,16},{120,24},{128,32},{136,40},{144,48},{152,5... | collective-permute-start | bytes 1769480 | tf_op jit(solution)/shard_map/ppermute | solution.py:14
  67.0 18.3 %collective-permute-done = bf16[384,3,256]{2,0,1:T(8,128)(2,1)} collective-permute-done((bf16[384,3,256]{2,0,1:T(8,128)(2,1)}, bf16[384,3,256]{2,0,1:T(8,128)(2,1)}, u32[]{:S(2)}, u32[]{:S(2)}) %collective-permute-start) | collective-permute-done | bytes 589856 | tf_op jit(solution)/shard_map/ppermute | solution.py:14
  85.3 6.3 collective-permute-start.5
  91.6 34.4 %collective-permute-done.1 = bf16[384,3,256]{2,0,1:T(8,128)(2,1)} collective-permute-done((bf16[384,3,256]{2,0,1:T(8,128)(2,1)}, bf16[384,3,256]{2,0,1:T(8,128)(2,1)}, u32[]{:S(2)}, u32[]{:S(2)}) %collective-permute-start.1) | collective-permute-done | bytes 589856 | tf_op jit(solution)/shard_map/ppermute | solution.py:14
  127.9 23.2 %collective-permute-done.2 = bf16[384,3,256]{2,0,1:T(8,128)(2,1)} collective-permute-done((bf16[384,3,256]{2,0,1:T(8,128)(2,1)}, bf16[384,3,256]{2,0,1:T(8,128)(2,1)}, u32[]{:S(2)}, u32[]{:S(2)}) %collective-permute-start.2) | collective-permute-done | bytes 589856 | tf_op jit(solution)/shard_map/ppermute | solution.py:14
  153.0 12.4 %collective-permute-done.3 = bf16[384,3,256]{2,0,1:T(8,128)(2,1)} collective-permute-done((bf16[384,3,256]{2,0,1:T(8,128)(2,1)}, bf16[384,3,256]{2,0,1:T(8,128)(2,1)}, u32[]{:S(2)}, u32[]{:S(2)}) %collective-permute-start.3) | collective-permute-done | bytes 589856 | tf_op jit(solution)/shard_map/ppermute | solution.py:14
  165.4 7.0 %collective-permute-start.8 = (bf16[384,3,256]{2,0,1:T(8,128)(2,1)}, bf16[384,3,256]{2,0,1:T(8,128)(2,1)}, u32[]{:S(2)}, u32[]{:S(2)}) collective-permute-start(bf16[384,3,256]{2,0,1:T(8,128)(2,1)} %slice.214), channel_id=1, source_target_pairs={{32,0},{40,8},{48,16},{56,24},{64,32},{72,40},{80,48},{88,56},{96,... | collective-permute-start | bytes 1769480 | tf_op jit(solution)/shard_map/ppermute | solution.py:14
  172.4 17.0 %collective-permute-start.9 = (bf16[384,3,256]{2,0,1:T(8,128)(2,1)}, bf16[384,3,256]{2,0,1:T(8,128)(2,1)}, u32[]{:S(2)}, u32[]{:S(2)}) collective-permute-start(bf16[384,3,256]{2,0,1:T(8,128)(2,1)} %slice.214), channel_id=1, source_target_pairs={{24,0},{32,8},{40,16},{48,24},{56,32},{64,40},{72,48},{80,56},{88,... | collective-permute-start | bytes 1769480 | tf_op jit(solution)/shard_map/ppermute | solution.py:14
  193.9 23.3 %collective-permute-done.7 = bf16[384,3,256]{2,0,1:T(8,128)(2,1)} collective-permute-done((bf16[384,3,256]{2,0,1:T(8,128)(2,1)}, bf16[384,3,256]{2,0,1:T(8,128)(2,1)}, u32[]{:S(2)}, u32[]{:S(2)}) %collective-permute-start.7) | collective-permute-done | bytes 589856 | tf_op jit(solution)/shard_map/ppermute | solution.py:14
  217.1 21.0 %collective-permute-start.12 = (bf16[384,3,256]{2,0,1:T(8,128)(2,1)}, bf16[384,3,256]{2,0,1:T(8,128)(2,1)}, u32[]{:S(2)}, u32[]{:S(2)}) collective-permute-start(bf16[384,3,256]{2,0,1:T(8,128)(2,1)} %slice.214), channel_id=1, source_target_pairs={{0,8},{8,16},{16,24},{24,32},{32,40},{40,48},{48,56},{56,64},{64,7... | collective-permute-start | bytes 1769480 | tf_op jit(solution)/shard_map/ppermute | solution.py:14
  238.1 12.1 %collective-permute-start.13 = (bf16[384,3,256]{2,0,1:T(8,128)(2,1)}, bf16[384,3,256]{2,0,1:T(8,128)(2,1)}, u32[]{:S(2)}, u32[]{:S(2)}) collective-permute-start(bf16[384,3,256]{2,0,1:T(8,128)(2,1)} %slice.214), channel_id=1, source_target_pairs={{0,16},{8,24},{16,32},{24,40},{32,48},{40,56},{48,64},{56,72},{64,... | collective-permute-start | bytes 1769480 | tf_op jit(solution)/shard_map/ppermute | solution.py:14
  250.2 21.8 %collective-permute-done.9 = bf16[384,3,256]{2,0,1:T(8,128)(2,1)} collective-permute-done((bf16[384,3,256]{2,0,1:T(8,128)(2,1)}, bf16[384,3,256]{2,0,1:T(8,128)(2,1)}, u32[]{:S(2)}, u32[]{:S(2)}) %collective-permute-start.9) | collective-permute-done | bytes 589856 | tf_op jit(solution)/shard_map/ppermute | solution.py:14
  272.0 27.5 %collective-permute-start.14 = (bf16[384,3,256]{2,0,1:T(8,128)(2,1)}, bf16[384,3,256]{2,0,1:T(8,128)(2,1)}, u32[]{:S(2)}, u32[]{:S(2)}) collective-permute-start(bf16[384,3,256]{2,0,1:T(8,128)(2,1)} %slice.214), channel_id=1, source_target_pairs={{0,24},{8,32},{16,40},{24,48},{32,56},{40,64},{48,72},{56,80},{64,... | collective-permute-start | bytes 1769480 | tf_op jit(solution)/shard_map/ppermute | solution.py:14
  299.5 64.9 %collective-permute-start.15 = (bf16[384,3,256]{2,0,1:T(8,128)(2,1)}, bf16[384,3,256]{2,0,1:T(8,128)(2,1)}, u32[]{:S(2)}, u32[]{:S(2)}) collective-permute-start(bf16[384,3,256]{2,0,1:T(8,128)(2,1)} %slice.214), channel_id=1, source_target_pairs={{0,32},{8,40},{16,48},{24,56},{32,64},{40,72},{48,80},{56,88},{64,... | collective-permute-start | bytes 1769480 | tf_op jit(solution)/shard_map/ppermute | solution.py:14
  364.4 11.6 %collective-permute-start.16 = (bf16[384,3,256]{2,0,1:T(8,128)(2,1)}, bf16[384,3,256]{2,0,1:T(8,128)(2,1)}, u32[]{:S(2)}, u32[]{:S(2)}) collective-permute-start(bf16[384,3,256]{2,0,1:T(8,128)(2,1)} %slice.214), channel_id=1, source_target_pairs={{0,40},{8,48},{16,56},{24,64},{32,72},{40,80},{48,88},{56,96},{64,... | collective-permute-start | bytes 1769480 | tf_op jit(solution)/shard_map/ppermute | solution.py:14
  381.9 7.5 %collective-permute-done.15 = bf16[384,3,256]{2,0,1:T(8,128)(2,1)} collective-permute-done((bf16[384,3,256]{2,0,1:T(8,128)(2,1)}, bf16[384,3,256]{2,0,1:T(8,128)(2,1)}, u32[]{:S(2)}, u32[]{:S(2)}) %collective-permute-start.15) | collective-permute-done | bytes 589856 | tf_op jit(solution)/shard_map/ppermute | solution.py:14
  391.2 26.1 %collective-permute-done.16 = bf16[384,3,256]{2,0,1:T(8,128)(2,1)} collective-permute-done((bf16[384,3,256]{2,0,1:T(8,128)(2,1)}, bf16[384,3,256]{2,0,1:T(8,128)(2,1)}, u32[]{:S(2)}, u32[]{:S(2)}) %collective-permute-start.16) | collective-permute-done | bytes 589856 | tf_op jit(solution)/shard_map/ppermute | solution.py:14
  417.3 13.9 %collective-permute-start.21 = (bf16[384,3,256]{2,0,1:T(8,128)(2,1)}, bf16[384,3,256]{2,0,1:T(8,128)(2,1)}, u32[]{:S(2)}, u32[]{:S(2)}) collective-permute-start(bf16[384,3,256]{2,0,1:T(8,128)(2,1)} %slice.214), channel_id=1, source_target_pairs={{0,80},{8,88},{16,96},{24,104},{32,112},{40,120},{48,128},{56,136}... | collective-permute-start | bytes 1769480 | tf_op jit(solution)/shard_map/ppermute | solution.py:14
  431.3 12.6 %collective-permute-done.17 = bf16[384,3,256]{2,0,1:T(8,128)(2,1)} collective-permute-done((bf16[384,3,256]{2,0,1:T(8,128)(2,1)}, bf16[384,3,256]{2,0,1:T(8,128)(2,1)}, u32[]{:S(2)}, u32[]{:S(2)}) %collective-permute-start.17) | collective-permute-done | bytes 589856 | tf_op jit(solution)/shard_map/ppermute | solution.py:14
  445.8 30.3 %collective-permute-done.18 = bf16[384,3,256]{2,0,1:T(8,128)(2,1)} collective-permute-done((bf16[384,3,256]{2,0,1:T(8,128)(2,1)}, bf16[384,3,256]{2,0,1:T(8,128)(2,1)}, u32[]{:S(2)}, u32[]{:S(2)}) %collective-permute-start.18) | collective-permute-done | bytes 589856 | tf_op jit(solution)/shard_map/ppermute | solution.py:14
  579.7 8.1 %conditional.34 = ((f32[3,384]{1,0:T(4,128)}, f32[3,384]{1,0:T(4,128)S(1)}, f32[3,384,128]{2,1,0:T(8,128)S(1)})) conditional(s32[]{:T(128)} %bitcast.106, (f32[3,384]{1,0:T(4,128)}, f32[3,384]{1,0:T(4,128)S(1)}, f32[3,384,128]{2,1,0:T(8,128)S(1)}) %get-tuple-element.1021, (pred[1]{0:T(512)(128)(4,1)}, bf16[384,3,256]{2,0,1:T(8,128)(2,1)}, ...), branch_computations={%region_38.39_spmd, %region_39.42_spmd} | conditional | flops 232540416 | bytes 7447585 | solution.py:80
  587.8 5.6 conditional.35
  593.4 6.3 conditional.37
  599.8 5.6 conditional.39
  605.4 5.6 conditional.40
  611.0 6.0 conditional.41
  617.0 5.6 conditional.43
  622.7 5.6 conditional.44
  628.3 5.6 conditional.45
  637.4 39.5 %reduce-scatter.2.cloned.1.call-done = bf16[48,3072]{1,0:T(8,128)(2,1)} async-done(((bf16[384,3072]{1,0:T(8,128)(2,1)}), bf16[48,3072]{1,0:T(8,128)(2,1)}) %reduce-scatter.2.cloned.1.call-update) | async-done | bytes 294928 | tf_op jit(solution)/shard_map/reduce_scatter | solution.py:101
  (126 shorter events, 99.4 us)
Async XLA Ops:
  6.5 627.9 %copy-start = (bf16[384,3072]{1,0:T(8,128)(2,1)S(1)}, bf16[384,3072]{1,0:T(8,128)(2,1)}, u32[]{:S(2)}) copy-start(bf16[384,3072]{1,0:T(8,128)(2,1)} %param.63) | copy-start | bytes 7077892
  6.5 36.4 %all-gather.2.cloned.1.call-start = ((), (), s32[]{:S(2)}) async-start(), calls=%async_computation.1 | async-start | bytes 2654208 | tf_op jit(solution)/shard_map/all_gather | solution.py:29
  11.6 466.4 %copy-start.2 = (s32[32]{0:T(128)S(1)}, s32[32]{0:T(128)}, u32[]{:S(2)}) copy-start(s32[32]{0:T(128)} %param.64) | copy-start | bytes 388
  11.6 469.6 %copy-start.4 = (s32[32,2]{0,1:T(2,128)S(1)}, s32[32,2]{0,1:T(2,128)}, u32[]{:S(2)}) copy-start(s32[32,2]{0,1:T(2,128)} %param.65) | copy-start | bytes 772
  11.6 665.2 %reduce-scatter.2.cloned.1.call-start = ((), (), s32[]{:S(2)}) async-start(), calls=%async_computation.2 | async-start | bytes 2654208 | tf_op jit(solution)/shard_map/reduce_scatter | solution.py:101
  49.8 0.9 copy-start.1
  51.6 33.7 %collective-permute-start = (bf16[384,3,256]{2,0,1:T(8,128)(2,1)}, bf16[384,3,256]{2,0,1:T(8,128)(2,1)}, u32[]{:S(2)}, u32[]{:S(2)}) collective-permute-start(bf16[384,3,256]{2,0,1:T(8,128)(2,1)} %slice.214), channel_id=1, source_target_pairs={{96,0},{104,8},{112,16},{120,24},{128,32},{136,40},{144,48},{152,5... | collective-permute-start | bytes 1769480 | tf_op jit(solution)/shard_map/ppermute | solution.py:14
  59.2 66.8 %collective-permute-start.1 = (bf16[384,3,256]{2,0,1:T(8,128)(2,1)}, bf16[384,3,256]{2,0,1:T(8,128)(2,1)}, u32[]{:S(2)}, u32[]{:S(2)}) collective-permute-start(bf16[384,3,256]{2,0,1:T(8,128)(2,1)} %slice.214), channel_id=1, source_target_pairs={{88,0},{96,8},{104,16},{112,24},{120,32},{128,40},{136,48},{144,56... | collective-permute-start | bytes 1769480 | tf_op jit(solution)/shard_map/ppermute | solution.py:14
  61.2 90.0 %collective-permute-start.2 = (bf16[384,3,256]{2,0,1:T(8,128)(2,1)}, bf16[384,3,256]{2,0,1:T(8,128)(2,1)}, u32[]{:S(2)}, u32[]{:S(2)}) collective-permute-start(bf16[384,3,256]{2,0,1:T(8,128)(2,1)} %slice.214), channel_id=1, source_target_pairs={{80,0},{88,8},{96,16},{104,24},{112,32},{120,40},{128,48},{136,56}... | collective-permute-start | bytes 1769480 | tf_op jit(solution)/shard_map/ppermute | solution.py:14
  63.1 102.3 %collective-permute-start.3 = (bf16[384,3,256]{2,0,1:T(8,128)(2,1)}, bf16[384,3,256]{2,0,1:T(8,128)(2,1)}, u32[]{:S(2)}, u32[]{:S(2)}) collective-permute-start(bf16[384,3,256]{2,0,1:T(8,128)(2,1)} %slice.214), channel_id=1, source_target_pairs={{72,0},{80,8},{88,16},{96,24},{104,32},{112,40},{120,48},{128,56},... | collective-permute-start | bytes 1769480 | tf_op jit(solution)/shard_map/ppermute | solution.py:14
  65.0 107.4 %collective-permute-start.4 = (bf16[384,3,256]{2,0,1:T(8,128)(2,1)}, bf16[384,3,256]{2,0,1:T(8,128)(2,1)}, u32[]{:S(2)}, u32[]{:S(2)}) collective-permute-start(bf16[384,3,256]{2,0,1:T(8,128)(2,1)} %slice.214), channel_id=1, source_target_pairs={{64,0},{72,8},{80,16},{88,24},{96,32},{104,40},{112,48},{120,56},{... | collective-permute-start | bytes 1769480 | tf_op jit(solution)/shard_map/ppermute | solution.py:14
  85.3 104.2 %collective-permute-start.5 = (bf16[384,3,256]{2,0,1:T(8,128)(2,1)}, bf16[384,3,256]{2,0,1:T(8,128)(2,1)}, u32[]{:S(2)}, u32[]{:S(2)}) collective-permute-start(bf16[384,3,256]{2,0,1:T(8,128)(2,1)} %slice.214), channel_id=1, source_target_pairs={{56,0},{64,8},{72,16},{80,24},{88,32},{96,40},{104,48},{112,56},{1... | collective-permute-start | bytes 1769480 | tf_op jit(solution)/shard_map/ppermute | solution.py:14
  126.0 65.4 %collective-permute-start.6 = (bf16[384,3,256]{2,0,1:T(8,128)(2,1)}, bf16[384,3,256]{2,0,1:T(8,128)(2,1)}, u32[]{:S(2)}, u32[]{:S(2)}) collective-permute-start(bf16[384,3,256]{2,0,1:T(8,128)(2,1)} %slice.214), channel_id=1, source_target_pairs={{48,0},{56,8},{64,16},{72,24},{80,32},{88,40},{96,48},{104,56},{11... | collective-permute-start | bytes 1769480 | tf_op jit(solution)/shard_map/ppermute | solution.py:14
  151.1 66.0 %collective-permute-start.7 = (bf16[384,3,256]{2,0,1:T(8,128)(2,1)}, bf16[384,3,256]{2,0,1:T(8,128)(2,1)}, u32[]{:S(2)}, u32[]{:S(2)}) collective-permute-start(bf16[384,3,256]{2,0,1:T(8,128)(2,1)} %slice.214), channel_id=1, source_target_pairs={{40,0},{48,8},{56,16},{64,24},{72,32},{80,40},{88,48},{96,56},{104... | collective-permute-start | bytes 1769480 | tf_op jit(solution)/shard_map/ppermute | solution.py:14
  165.4 72.7 %collective-permute-start.8 = (bf16[384,3,256]{2,0,1:T(8,128)(2,1)}, bf16[384,3,256]{2,0,1:T(8,128)(2,1)}, u32[]{:S(2)}, u32[]{:S(2)}) collective-permute-start(bf16[384,3,256]{2,0,1:T(8,128)(2,1)} %slice.214), channel_id=1, source_target_pairs={{32,0},{40,8},{48,16},{56,24},{64,32},{72,40},{80,48},{88,56},{96,... | collective-permute-start | bytes 1769480 | tf_op jit(solution)/shard_map/ppermute | solution.py:14
  172.4 99.6 %collective-permute-start.9 = (bf16[384,3,256]{2,0,1:T(8,128)(2,1)}, bf16[384,3,256]{2,0,1:T(8,128)(2,1)}, u32[]{:S(2)}, u32[]{:S(2)}) collective-permute-start(bf16[384,3,256]{2,0,1:T(8,128)(2,1)} %slice.214), channel_id=1, source_target_pairs={{24,0},{32,8},{40,16},{48,24},{56,32},{64,40},{72,48},{80,56},{88,... | collective-permute-start | bytes 1769480 | tf_op jit(solution)/shard_map/ppermute | solution.py:14
  189.4 110.1 %collective-permute-start.10 = (bf16[384,3,256]{2,0,1:T(8,128)(2,1)}, bf16[384,3,256]{2,0,1:T(8,128)(2,1)}, u32[]{:S(2)}, u32[]{:S(2)}) collective-permute-start(bf16[384,3,256]{2,0,1:T(8,128)(2,1)} %slice.214), channel_id=1, source_target_pairs={{16,0},{24,8},{32,16},{40,24},{48,32},{56,40},{64,48},{72,56},{80,... | collective-permute-start | bytes 1769480 | tf_op jit(solution)/shard_map/ppermute | solution.py:14
  191.4 173.0 %collective-permute-start.11 = (bf16[384,3,256]{2,0,1:T(8,128)(2,1)}, bf16[384,3,256]{2,0,1:T(8,128)(2,1)}, u32[]{:S(2)}, u32[]{:S(2)}) collective-permute-start(bf16[384,3,256]{2,0,1:T(8,128)(2,1)} %slice.214), channel_id=1, source_target_pairs={{8,0},{16,8},{24,16},{32,24},{40,32},{48,40},{56,48},{64,56},{72,6... | collective-permute-start | bytes 1769480 | tf_op jit(solution)/shard_map/ppermute | solution.py:14
  217.1 158.9 %collective-permute-start.12 = (bf16[384,3,256]{2,0,1:T(8,128)(2,1)}, bf16[384,3,256]{2,0,1:T(8,128)(2,1)}, u32[]{:S(2)}, u32[]{:S(2)}) collective-permute-start(bf16[384,3,256]{2,0,1:T(8,128)(2,1)} %slice.214), channel_id=1, source_target_pairs={{0,8},{8,16},{16,24},{24,32},{32,40},{40,48},{48,56},{56,64},{64,7... | collective-permute-start | bytes 1769480 | tf_op jit(solution)/shard_map/ppermute | solution.py:14
  238.1 139.8 %collective-permute-start.13 = (bf16[384,3,256]{2,0,1:T(8,128)(2,1)}, bf16[384,3,256]{2,0,1:T(8,128)(2,1)}, u32[]{:S(2)}, u32[]{:S(2)}) collective-permute-start(bf16[384,3,256]{2,0,1:T(8,128)(2,1)} %slice.214), channel_id=1, source_target_pairs={{0,16},{8,24},{16,32},{24,40},{32,48},{40,56},{48,64},{56,72},{64,... | collective-permute-start | bytes 1769480 | tf_op jit(solution)/shard_map/ppermute | solution.py:14
  272.0 107.9 %collective-permute-start.14 = (bf16[384,3,256]{2,0,1:T(8,128)(2,1)}, bf16[384,3,256]{2,0,1:T(8,128)(2,1)}, u32[]{:S(2)}, u32[]{:S(2)}) collective-permute-start(bf16[384,3,256]{2,0,1:T(8,128)(2,1)} %slice.214), channel_id=1, source_target_pairs={{0,24},{8,32},{16,40},{24,48},{32,56},{40,64},{48,72},{56,80},{64,... | collective-permute-start | bytes 1769480 | tf_op jit(solution)/shard_map/ppermute | solution.py:14
  299.5 89.8 %collective-permute-start.15 = (bf16[384,3,256]{2,0,1:T(8,128)(2,1)}, bf16[384,3,256]{2,0,1:T(8,128)(2,1)}, u32[]{:S(2)}, u32[]{:S(2)}) collective-permute-start(bf16[384,3,256]{2,0,1:T(8,128)(2,1)} %slice.214), channel_id=1, source_target_pairs={{0,32},{8,40},{16,48},{24,56},{32,64},{40,72},{48,80},{56,88},{64,... | collective-permute-start | bytes 1769480 | tf_op jit(solution)/shard_map/ppermute | solution.py:14
  364.4 52.9 %collective-permute-start.16 = (bf16[384,3,256]{2,0,1:T(8,128)(2,1)}, bf16[384,3,256]{2,0,1:T(8,128)(2,1)}, u32[]{:S(2)}, u32[]{:S(2)}) collective-permute-start(bf16[384,3,256]{2,0,1:T(8,128)(2,1)} %slice.214), channel_id=1, source_target_pairs={{0,40},{8,48},{16,56},{24,64},{32,72},{40,80},{48,88},{56,96},{64,... | collective-permute-start | bytes 1769480 | tf_op jit(solution)/shard_map/ppermute | solution.py:14
  376.0 67.8 %collective-permute-start.17 = (bf16[384,3,256]{2,0,1:T(8,128)(2,1)}, bf16[384,3,256]{2,0,1:T(8,128)(2,1)}, u32[]{:S(2)}, u32[]{:S(2)}) collective-permute-start(bf16[384,3,256]{2,0,1:T(8,128)(2,1)} %slice.214), channel_id=1, source_target_pairs={{0,48},{8,56},{16,64},{24,72},{32,80},{40,88},{48,96},{56,104},{64... | collective-permute-start | bytes 1769480 | tf_op jit(solution)/shard_map/ppermute | solution.py:14
  378.0 98.1 %collective-permute-start.18 = (bf16[384,3,256]{2,0,1:T(8,128)(2,1)}, bf16[384,3,256]{2,0,1:T(8,128)(2,1)}, u32[]{:S(2)}, u32[]{:S(2)}) collective-permute-start(bf16[384,3,256]{2,0,1:T(8,128)(2,1)} %slice.214), channel_id=1, source_target_pairs={{0,56},{8,64},{16,72},{24,80},{32,88},{40,96},{48,104},{56,112},{6... | collective-permute-start | bytes 1769480 | tf_op jit(solution)/shard_map/ppermute | solution.py:14
  379.9 248.4 %collective-permute-start.19 = (bf16[384,3,256]{2,0,1:T(8,128)(2,1)}, bf16[384,3,256]{2,0,1:T(8,128)(2,1)}, u32[]{:S(2)}, u32[]{:S(2)}) collective-permute-start(bf16[384,3,256]{2,0,1:T(8,128)(2,1)} %slice.214), channel_id=1, source_target_pairs={{0,64},{8,72},{16,80},{24,88},{32,96},{40,104},{48,112},{56,120},{... | collective-permute-start | bytes 1769480 | tf_op jit(solution)/shard_map/ppermute | solution.py:14
  389.3 244.6 %collective-permute-start.20 = (bf16[384,3,256]{2,0,1:T(8,128)(2,1)}, bf16[384,3,256]{2,0,1:T(8,128)(2,1)}, u32[]{:S(2)}, u32[]{:S(2)}) collective-permute-start(bf16[384,3,256]{2,0,1:T(8,128)(2,1)} %slice.214), channel_id=1, source_target_pairs={{0,72},{8,80},{16,88},{24,96},{32,104},{40,112},{48,120},{56,128},... | collective-permute-start | bytes 1769480 | tf_op jit(solution)/shard_map/ppermute | solution.py:14
  417.3 216.6 %collective-permute-start.21 = (bf16[384,3,256]{2,0,1:T(8,128)(2,1)}, bf16[384,3,256]{2,0,1:T(8,128)(2,1)}, u32[]{:S(2)}, u32[]{:S(2)}) collective-permute-start(bf16[384,3,256]{2,0,1:T(8,128)(2,1)} %slice.214), channel_id=1, source_target_pairs={{0,80},{8,88},{16,96},{24,104},{32,112},{40,120},{48,128},{56,136}... | collective-permute-start | bytes 1769480 | tf_op jit(solution)/shard_map/ppermute | solution.py:14
  443.8 190.1 %collective-permute-start.22 = (bf16[384,3,256]{2,0,1:T(8,128)(2,1)}, bf16[384,3,256]{2,0,1:T(8,128)(2,1)}, u32[]{:S(2)}, u32[]{:S(2)}) collective-permute-start(bf16[384,3,256]{2,0,1:T(8,128)(2,1)} %slice.214), channel_id=1, source_target_pairs={{0,88},{8,96},{16,104},{24,112},{32,120},{40,128},{48,136},{56,144... | collective-permute-start | bytes 1769480 | tf_op jit(solution)/shard_map/ppermute | solution.py:14
  476.1 158.1 %collective-permute-start.23 = (bf16[384,3,256]{2,0,1:T(8,128)(2,1)}, bf16[384,3,256]{2,0,1:T(8,128)(2,1)}, u32[]{:S(2)}, u32[]{:S(2)}) collective-permute-start(bf16[384,3,256]{2,0,1:T(8,128)(2,1)} %slice.214), channel_id=1, source_target_pairs={{0,96},{8,104},{16,112},{24,120},{32,128},{40,136},{48,144},{56,15... | collective-permute-start | bytes 1769480 | tf_op jit(solution)/shard_map/ppermute | solution.py:14
  637.3 39.5 %copy-start.3 = (f32[3072]{0:T(1024)S(1)}, f32[3072]{0:T(1024)}, u32[]{:S(2)}) copy-start(f32[3072]{0:T(1024)} %param.61) | copy-start | bytes 36868
Sparse Core Ops, SparseCore 0:
  11.7 31.0 all-gather.1
  637.5 39.3 reduce-scatter.1
where the time goes:
time: 697 us; the launch traced here: 686 us
  waiting for transfers between devices  281 us (40%)
  starting transfers between devices  216 us (31%)
  between operations  107 us (15%)
  matrix products  38.1 us (5%)
  other arithmetic  25.2 us (4%)
  local copies, waits for them, and re-layouts  9.26 us (1%)
  loops' own time  9.18 us (1%)
    ppermute x24, starting transfers between devices, from_behind(): return lax.ppermute(block, axis, route)  216 us
    ppermute x24, waiting for transfers between devices, from_behind(): return lax.ppermute(block, axis, route)  210 us
    reduce_scatter x1, waiting for transfers between devices, on_device(): lax.psum_scatter(jnp.dot(attn, w_out, preferred_element_type=jnp.float32)...  39.5 us
    all_gather x1, waiting for transfers between devices, on_device(): lax.all_gather(normed, 'uly', axis=0, tiled=True)  31.2 us
    dot_general x9, matrix products, compute(): jnp.einsum('hqk,khd->hqd', weights, kv_tile[:, :, head_dim:], preferred_e...  15.8 us
  transfers between devices with their start and end apart: 26, of which 12 were waited for; matrix products, arithmetic and copies ran while one was open for 8% of the time, Pallas kernels for 0%

commit v1 on v0

--- a/solution.py
+++ b/solution.py
@@ -6,6 +6,14 @@
 TILE = 384
 WIN = 3
 GW = 4
+
+
+def tiled_gather(shard, axis, dim):
+    size = lax.axis_size(axis)
+    repeats = [size if d == dim else 1 for d in range(shard.ndim)]
+    return lax.all_to_all(
+        jnp.tile(shard, repeats), axis, split_axis=dim, concat_axis=dim, tiled=True
+    )
 
 
 def from_behind(block, axis, distance):
@@ -25,10 +33,7 @@
     heads_dev = w_qkv.shape[1]
     head_dim = w_qkv.shape[2] // 3
     qkv = jnp.einsum(
-        "td,dhe->the",
-        lax.all_gather(normed, "uly", axis=0, tiled=True),
-        w_qkv,
-        preferred_element_type=jnp.float32,
+        "td,dhe->the", tiled_gather(normed, "uly", 0), w_qkv, preferred_element_type=jnp.float32
     ).astype(jnp.bfloat16)
     group_rows = qkv.shape[0]
     tiles_here = group_rows // TILE

time: 697 us -> 670 us (0.961)
  starting transfers between devices: 216 us -> 168 us
  blocking collectives: 0 us -> 34.9 us
  waiting for transfers between devices: 281 us -> 273 us
    ppermute x24, starting transfers between devices: 216 us -> 168 us  [from_behind(): return lax.ppermute(block, axis, route)]
    all_to_all x0 -> x1, blocking collectives: none -> 34.9 us  [tiled_gather(): lax.all_to_all(jnp.tile(shard, repeats), axis, split_axis=dim, concat_axi...]
    all_gather x1 -> x0, waiting for transfers between devices: 31.2 us -> none  [on_device(): lax.all_gather(normed, 'uly', axis=0, tiled=True)]
    reduce_scatter x1, waiting for transfers between devices: 39.5 us -> 59.5 us  [on_device(): lax.psum_scatter(jnp.dot(attn, w_out, preferred_element_type=jnp.float32)...]
  transfers between devices with their start and end apart: 26 -> 25, of which waited for: 12 -> 11; matrix products, arithmetic and copies ran while one was open for 8% -> 8% of each run, Pallas kernels for 0% -> 0%
where the time goes in v1:
time: 670 us; the launch traced here: 659 us
  waiting for transfers between devices  273 us (41%)
  starting transfers between devices  168 us (25%)
  between operations  106 us (16%)
  blocking collectives  34.9 us (5%)
  matrix products  34.4 us (5%)
  other arithmetic  24.5 us (4%)
  local copies, waits for them, and re-layouts  9.49 us (1%)
  loops' own time  9.06 us (1%)
    ppermute x24, waiting for transfers between devices, from_behind(): return lax.ppermute(block, axis, route)  213 us
    ppermute x24, starting transfers between devices, from_behind(): return lax.ppermute(block, axis, route)  168 us
    reduce_scatter x1, waiting for transfers between devices, on_device(): lax.psum_scatter(jnp.dot(attn, w_out, preferred_element_type=jnp.float32)...  59.5 us
    all_to_all x1, blocking collectives, tiled_gather(): lax.all_to_all(jnp.tile(shard, repeats), axis, split_axis=dim, concat_axi...  34.9 us
    dot_general x9, matrix products, compute(): jnp.einsum('hqk,khd->hqd', weights, kv_tile[:, :, head_dim:], preferred_e...  15.8 us
  transfers between devices with their start and end apart: 25, of which 11 were waited for; matrix products, arithmetic and copies ran while one was open for 8% of the time, Pallas kernels for 0%

profile of v1, /device:TPU:4, one launch (start us, length us, event | category | flops | bytes accessed | tf_op | source)
XLA Modules:
  0.0 659.0 jit_solution(14448534223743909291)
XLA Ops:
  11.2 34.9 %all_to_all.9 = bf16[8,48,3072]{2,1,0:T(8,128)(2,1)S(1)} all-to-all(bf16[8,48,3072]{2,1,0:T(8,128)(2,1)S(1)} %tile.2), channel_id=1, replica_groups=mesh['blk'=32,'uly'=8] {'uly'}, dimensions={0} | all-to-all | bytes 4718592 | tf_op jit(solution)/shard_map/all_to_all | solution.py:14
  51.1 9.0 %collective-permute-start = (bf16[384,3,256]{2,0,1:T(8,128)(2,1)}, bf16[384,3,256]{2,0,1:T(8,128)(2,1)}, u32[]{:S(2)}, u32[]{:S(2)}) collective-permute-start(bf16[384,3,256]{2,0,1:T(8,128)(2,1)} %slice.214), channel_id=1, source_target_pairs={{96,0},{104,8},{112,16},{120,24},{128,32},{136,40},{144,48},{152,5... | collective-permute-start | bytes 1769480 | tf_op jit(solution)/shard_map/ppermute | solution.py:22
  67.9 17.7 %collective-permute-done = bf16[384,3,256]{2,0,1:T(8,128)(2,1)} collective-permute-done((bf16[384,3,256]{2,0,1:T(8,128)(2,1)}, bf16[384,3,256]{2,0,1:T(8,128)(2,1)}, u32[]{:S(2)}, u32[]{:S(2)}) %collective-permute-start) | collective-permute-done | bytes 589856 | tf_op jit(solution)/shard_map/ppermute | solution.py:22
  85.6 7.6 %collective-permute-start.5 = (bf16[384,3,256]{2,0,1:T(8,128)(2,1)}, bf16[384,3,256]{2,0,1:T(8,128)(2,1)}, u32[]{:S(2)}, u32[]{:S(2)}) collective-permute-start(bf16[384,3,256]{2,0,1:T(8,128)(2,1)} %slice.214), channel_id=1, source_target_pairs={{56,0},{64,8},{72,16},{80,24},{88,32},{96,40},{104,48},{112,56},{1... | collective-permute-start | bytes 1769480 | tf_op jit(solution)/shard_map/ppermute | solution.py:22
  93.2 33.0 %collective-permute-done.1 = bf16[384,3,256]{2,0,1:T(8,128)(2,1)} collective-permute-done((bf16[384,3,256]{2,0,1:T(8,128)(2,1)}, bf16[384,3,256]{2,0,1:T(8,128)(2,1)}, u32[]{:S(2)}, u32[]{:S(2)}) %collective-permute-start.1) | collective-permute-done | bytes 589856 | tf_op jit(solution)/shard_map/ppermute | solution.py:22
  128.1 21.5 %collective-permute-done.2 = bf16[384,3,256]{2,0,1:T(8,128)(2,1)} collective-permute-done((bf16[384,3,256]{2,0,1:T(8,128)(2,1)}, bf16[384,3,256]{2,0,1:T(8,128)(2,1)}, u32[]{:S(2)}, u32[]{:S(2)}) %collective-permute-start.2) | collective-permute-done | bytes 589856 | tf_op jit(solution)/shard_map/ppermute | solution.py:22
  151.5 13.0 %collective-permute-done.3 = bf16[384,3,256]{2,0,1:T(8,128)(2,1)} collective-permute-done((bf16[384,3,256]{2,0,1:T(8,128)(2,1)}, bf16[384,3,256]{2,0,1:T(8,128)(2,1)}, u32[]{:S(2)}, u32[]{:S(2)}) %collective-permute-start.3) | collective-permute-done | bytes 589856 | tf_op jit(solution)/shard_map/ppermute | solution.py:22
  164.5 5.3 collective-permute-start.8
  169.8 44.7 %collective-permute-start.9 = (bf16[384,3,256]{2,0,1:T(8,128)(2,1)}, bf16[384,3,256]{2,0,1:T(8,128)(2,1)}, u32[]{:S(2)}, u32[]{:S(2)}) collective-permute-start(bf16[384,3,256]{2,0,1:T(8,128)(2,1)} %slice.214), channel_id=1, source_target_pairs={{24,0},{32,8},{40,16},{48,24},{56,32},{64,40},{72,48},{80,56},{88,... | collective-permute-start | bytes 1769480 | tf_op jit(solution)/shard_map/ppermute | solution.py:22
  219.0 8.9 %collective-permute-start.12 = (bf16[384,3,256]{2,0,1:T(8,128)(2,1)}, bf16[384,3,256]{2,0,1:T(8,128)(2,1)}, u32[]{:S(2)}, u32[]{:S(2)}) collective-permute-start(bf16[384,3,256]{2,0,1:T(8,128)(2,1)} %slice.214), channel_id=1, source_target_pairs={{0,8},{8,16},{16,24},{24,32},{32,40},{40,48},{48,56},{56,64},{64,7... | collective-permute-start | bytes 1769480 | tf_op jit(solution)/shard_map/ppermute | solution.py:22
  227.9 5.8 collective-permute-done.8
  233.6 9.2 %collective-permute-start.13 = (bf16[384,3,256]{2,0,1:T(8,128)(2,1)}, bf16[384,3,256]{2,0,1:T(8,128)(2,1)}, u32[]{:S(2)}, u32[]{:S(2)}) collective-permute-start(bf16[384,3,256]{2,0,1:T(8,128)(2,1)} %slice.214), channel_id=1, source_target_pairs={{0,16},{8,24},{16,32},{24,40},{32,48},{40,56},{48,64},{56,72},{64,... | collective-permute-start | bytes 1769480 | tf_op jit(solution)/shard_map/ppermute | solution.py:22
  242.8 13.9 %collective-permute-done.9 = bf16[384,3,256]{2,0,1:T(8,128)(2,1)} collective-permute-done((bf16[384,3,256]{2,0,1:T(8,128)(2,1)}, bf16[384,3,256]{2,0,1:T(8,128)(2,1)}, u32[]{:S(2)}, u32[]{:S(2)}) %collective-permute-start.9) | collective-permute-done | bytes 589856 | tf_op jit(solution)/shard_map/ppermute | solution.py:22
  256.8 8.5 %collective-permute-start.14 = (bf16[384,3,256]{2,0,1:T(8,128)(2,1)}, bf16[384,3,256]{2,0,1:T(8,128)(2,1)}, u32[]{:S(2)}, u32[]{:S(2)}) collective-permute-start(bf16[384,3,256]{2,0,1:T(8,128)(2,1)} %slice.214), channel_id=1, source_target_pairs={{0,24},{8,32},{16,40},{24,48},{32,56},{40,64},{48,72},{56,80},{64,... | collective-permute-start | bytes 1769480 | tf_op jit(solution)/shard_map/ppermute | solution.py:22
  265.3 19.2 %collective-permute-done.10 = bf16[384,3,256]{2,0,1:T(8,128)(2,1)} collective-permute-done((bf16[384,3,256]{2,0,1:T(8,128)(2,1)}, bf16[384,3,256]{2,0,1:T(8,128)(2,1)}, u32[]{:S(2)}, u32[]{:S(2)}) %collective-permute-start.10) | collective-permute-done | bytes 589856 | tf_op jit(solution)/shard_map/ppermute | solution.py:22
  284.5 4.6 collective-permute-start.15
  289.1 39.6 %collective-permute-done.11 = bf16[384,3,256]{2,0,1:T(8,128)(2,1)} collective-permute-done((bf16[384,3,256]{2,0,1:T(8,128)(2,1)}, bf16[384,3,256]{2,0,1:T(8,128)(2,1)}, u32[]{:S(2)}, u32[]{:S(2)}) %collective-permute-start.11) | collective-permute-done | bytes 589856 | tf_op jit(solution)/shard_map/ppermute | solution.py:22
  330.6 30.7 %collective-permute-start.17 = (bf16[384,3,256]{2,0,1:T(8,128)(2,1)}, bf16[384,3,256]{2,0,1:T(8,128)(2,1)}, u32[]{:S(2)}, u32[]{:S(2)}) collective-permute-start(bf16[384,3,256]{2,0,1:T(8,128)(2,1)} %slice.214), channel_id=1, source_target_pairs={{0,48},{8,56},{16,64},{24,72},{32,80},{40,88},{48,96},{56,104},{64... | collective-permute-start | bytes 1769480 | tf_op jit(solution)/shard_map/ppermute | solution.py:22
  361.3 11.6 %collective-permute-start.18 = (bf16[384,3,256]{2,0,1:T(8,128)(2,1)}, bf16[384,3,256]{2,0,1:T(8,128)(2,1)}, u32[]{:S(2)}, u32[]{:S(2)}) collective-permute-start(bf16[384,3,256]{2,0,1:T(8,128)(2,1)} %slice.214), channel_id=1, source_target_pairs={{0,56},{8,64},{16,72},{24,80},{32,88},{40,96},{48,104},{56,112},{6... | collective-permute-start | bytes 1769480 | tf_op jit(solution)/shard_map/ppermute | solution.py:22
  378.8 18.6 %collective-permute-done.17 = bf16[384,3,256]{2,0,1:T(8,128)(2,1)} collective-permute-done((bf16[384,3,256]{2,0,1:T(8,128)(2,1)}, bf16[384,3,256]{2,0,1:T(8,128)(2,1)}, u32[]{:S(2)}, u32[]{:S(2)}) %collective-permute-start.17) | collective-permute-done | bytes 589856 | tf_op jit(solution)/shard_map/ppermute | solution.py:22
  399.4 31.0 %collective-permute-done.18 = bf16[384,3,256]{2,0,1:T(8,128)(2,1)} collective-permute-done((bf16[384,3,256]{2,0,1:T(8,128)(2,1)}, bf16[384,3,256]{2,0,1:T(8,128)(2,1)}, u32[]{:S(2)}, u32[]{:S(2)}) %collective-permute-start.18) | collective-permute-done | bytes 589856 | tf_op jit(solution)/shard_map/ppermute | solution.py:22
  527.5 5.5 conditional.25
  533.3 8.1 %conditional.34 = ((f32[3,384]{1,0:T(4,128)}, f32[3,384]{1,0:T(4,128)S(1)}, f32[3,384,128]{2,1,0:T(8,128)S(1)})) conditional(s32[]{:T(128)} %bitcast.106, (f32[3,384]{1,0:T(4,128)}, f32[3,384]{1,0:T(4,128)S(1)}, f32[3,384,128]{2,1,0:T(8,128)S(1)}) %get-tuple-element.1021, (pred[1]{0:T(512)(128)(4,1)}, bf16[384,3,256]{2,0,1:T(8,128)(2,1)}, ...), branch_computations={%region_38.39_spmd, %region_39.42_spmd} | conditional | flops 232540416 | bytes 7447585 | solution.py:85
  541.4 5.6 conditional.35
  547.0 6.3 conditional.37
  553.3 5.6 conditional.39
  558.9 5.6 conditional.40
  564.5 6.0 conditional.41
  570.5 5.6 conditional.43
  576.1 5.6 conditional.44
  581.7 5.6 conditional.45
  590.7 59.5 %reduce-scatter.2.cloned.1.call-done = bf16[48,3072]{1,0:T(8,128)(2,1)} async-done(((bf16[384,3072]{1,0:T(8,128)(2,1)}), bf16[48,3072]{1,0:T(8,128)(2,1)}) %reduce-scatter.2.cloned.1.call-update) | async-done | bytes 294928 | tf_op jit(solution)/shard_map/reduce_scatter | solution.py:106
  (127 shorter events, 96.5 us)
Async XLA Ops:
  6.5 581.3 %copy-start = (bf16[384,3072]{1,0:T(8,128)(2,1)S(1)}, bf16[384,3072]{1,0:T(8,128)(2,1)}, u32[]{:S(2)}) copy-start(bf16[384,3072]{1,0:T(8,128)(2,1)} %param.63) | copy-start | bytes 7077892
  6.5 643.7 %reduce-scatter.2.cloned.1.call-start = ((), (), s32[]{:S(2)}) async-start(), calls=%async_computation.2 | async-start | bytes 2654208 | tf_op jit(solution)/shard_map/reduce_scatter | solution.py:106
  10.9 35.2 %copy-start.5 = (bf16[3072,3,384]{2,0,1:T(8,128)(2,1)S(1)}, bf16[3072,3,384]{2,0,1:T(8,128)(2,1)}, u32[]{:S(2)}) copy-start(bf16[3072,3,384]{2,0,1:T(8,128)(2,1)} %param.62) | copy-start | bytes 21233668
  46.1 386.3 %copy-start.2 = (s32[32]{0:T(128)S(1)}, s32[32]{0:T(128)}, u32[]{:S(2)}) copy-start(s32[32]{0:T(128)} %param.64) | copy-start | bytes 388
  46.1 389.7 %copy-start.4 = (s32[32,2]{0,1:T(2,128)S(1)}, s32[32,2]{0,1:T(2,128)}, u32[]{:S(2)}) copy-start(s32[32,2]{0,1:T(2,128)} %param.65) | copy-start | bytes 772
  49.3 0.9 copy-start.1
  51.1 34.4 %collective-permute-start = (bf16[384,3,256]{2,0,1:T(8,128)(2,1)}, bf16[384,3,256]{2,0,1:T(8,128)(2,1)}, u32[]{:S(2)}, u32[]{:S(2)}) collective-permute-start(bf16[384,3,256]{2,0,1:T(8,128)(2,1)} %slice.214), channel_id=1, source_target_pairs={{96,0},{104,8},{112,16},{120,24},{128,32},{136,40},{144,48},{152,5... | collective-permute-start | bytes 1769480 | tf_op jit(solution)/shard_map/ppermute | solution.py:22
  60.2 66.0 %collective-permute-start.1 = (bf16[384,3,256]{2,0,1:T(8,128)(2,1)}, bf16[384,3,256]{2,0,1:T(8,128)(2,1)}, u32[]{:S(2)}, u32[]{:S(2)}) collective-permute-start(bf16[384,3,256]{2,0,1:T(8,128)(2,1)} %slice.214), channel_id=1, source_target_pairs={{88,0},{96,8},{104,16},{112,24},{120,32},{128,40},{136,48},{144,56... | collective-permute-start | bytes 1769480 | tf_op jit(solution)/shard_map/ppermute | solution.py:22
  62.1 87.5 %collective-permute-start.2 = (bf16[384,3,256]{2,0,1:T(8,128)(2,1)}, bf16[384,3,256]{2,0,1:T(8,128)(2,1)}, u32[]{:S(2)}, u32[]{:S(2)}) collective-permute-start(bf16[384,3,256]{2,0,1:T(8,128)(2,1)} %slice.214), channel_id=1, source_target_pairs={{80,0},{88,8},{96,16},{104,24},{112,32},{120,40},{128,48},{136,56}... | collective-permute-start | bytes 1769480 | tf_op jit(solution)/shard_map/ppermute | solution.py:22
  64.0 100.5 %collective-permute-start.3 = (bf16[384,3,256]{2,0,1:T(8,128)(2,1)}, bf16[384,3,256]{2,0,1:T(8,128)(2,1)}, u32[]{:S(2)}, u32[]{:S(2)}) collective-permute-start(bf16[384,3,256]{2,0,1:T(8,128)(2,1)} %slice.214), channel_id=1, source_target_pairs={{72,0},{80,8},{88,16},{96,24},{104,32},{112,40},{120,48},{128,56},... | collective-permute-start | bytes 1769480 | tf_op jit(solution)/shard_map/ppermute | solution.py:22
  65.9 103.8 %collective-permute-start.4 = (bf16[384,3,256]{2,0,1:T(8,128)(2,1)}, bf16[384,3,256]{2,0,1:T(8,128)(2,1)}, u32[]{:S(2)}, u32[]{:S(2)}) collective-permute-start(bf16[384,3,256]{2,0,1:T(8,128)(2,1)} %slice.214), channel_id=1, source_target_pairs={{64,0},{72,8},{80,16},{88,24},{96,32},{104,40},{112,48},{120,56},{... | collective-permute-start | bytes 1769480 | tf_op jit(solution)/shard_map/ppermute | solution.py:22
  85.6 129.0 %collective-permute-start.5 = (bf16[384,3,256]{2,0,1:T(8,128)(2,1)}, bf16[384,3,256]{2,0,1:T(8,128)(2,1)}, u32[]{:S(2)}, u32[]{:S(2)}) collective-permute-start(bf16[384,3,256]{2,0,1:T(8,128)(2,1)} %slice.214), channel_id=1, source_target_pairs={{56,0},{64,8},{72,16},{80,24},{88,32},{96,40},{104,48},{112,56},{1... | collective-permute-start | bytes 1769480 | tf_op jit(solution)/shard_map/ppermute | solution.py:22
  126.1 90.3 %collective-permute-start.6 = (bf16[384,3,256]{2,0,1:T(8,128)(2,1)}, bf16[384,3,256]{2,0,1:T(8,128)(2,1)}, u32[]{:S(2)}, u32[]{:S(2)}) collective-permute-start(bf16[384,3,256]{2,0,1:T(8,128)(2,1)} %slice.214), channel_id=1, source_target_pairs={{48,0},{56,8},{64,16},{72,24},{80,32},{88,40},{96,48},{104,56},{11... | collective-permute-start | bytes 1769480 | tf_op jit(solution)/shard_map/ppermute | solution.py:22
  149.6 69.4 %collective-permute-start.7 = (bf16[384,3,256]{2,0,1:T(8,128)(2,1)}, bf16[384,3,256]{2,0,1:T(8,128)(2,1)}, u32[]{:S(2)}, u32[]{:S(2)}) collective-permute-start(bf16[384,3,256]{2,0,1:T(8,128)(2,1)} %slice.214), channel_id=1, source_target_pairs={{40,0},{48,8},{56,16},{64,24},{72,32},{80,40},{88,48},{96,56},{104... | collective-permute-start | bytes 1769480 | tf_op jit(solution)/shard_map/ppermute | solution.py:22
  164.5 69.2 %collective-permute-start.8 = (bf16[384,3,256]{2,0,1:T(8,128)(2,1)}, bf16[384,3,256]{2,0,1:T(8,128)(2,1)}, u32[]{:S(2)}, u32[]{:S(2)}) collective-permute-start(bf16[384,3,256]{2,0,1:T(8,128)(2,1)} %slice.214), channel_id=1, source_target_pairs={{32,0},{40,8},{48,16},{56,24},{64,32},{72,40},{80,48},{88,56},{96,... | collective-permute-start | bytes 1769480 | tf_op jit(solution)/shard_map/ppermute | solution.py:22
  169.8 87.0 %collective-permute-start.9 = (bf16[384,3,256]{2,0,1:T(8,128)(2,1)}, bf16[384,3,256]{2,0,1:T(8,128)(2,1)}, u32[]{:S(2)}, u32[]{:S(2)}) collective-permute-start(bf16[384,3,256]{2,0,1:T(8,128)(2,1)} %slice.214), channel_id=1, source_target_pairs={{24,0},{32,8},{40,16},{48,24},{56,32},{64,40},{72,48},{80,56},{88,... | collective-permute-start | bytes 1769480 | tf_op jit(solution)/shard_map/ppermute | solution.py:22
  214.5 70.0 %collective-permute-start.10 = (bf16[384,3,256]{2,0,1:T(8,128)(2,1)}, bf16[384,3,256]{2,0,1:T(8,128)(2,1)}, u32[]{:S(2)}, u32[]{:S(2)}) collective-permute-start(bf16[384,3,256]{2,0,1:T(8,128)(2,1)} %slice.214), channel_id=1, source_target_pairs={{16,0},{24,8},{32,16},{40,24},{48,32},{56,40},{64,48},{72,56},{80,... | collective-permute-start | bytes 1769480 | tf_op jit(solution)/shard_map/ppermute | solution.py:22
  216.5 112.2 %collective-permute-start.11 = (bf16[384,3,256]{2,0,1:T(8,128)(2,1)}, bf16[384,3,256]{2,0,1:T(8,128)(2,1)}, u32[]{:S(2)}, u32[]{:S(2)}) collective-permute-start(bf16[384,3,256]{2,0,1:T(8,128)(2,1)} %slice.214), channel_id=1, source_target_pairs={{8,0},{16,8},{24,16},{32,24},{40,32},{48,40},{56,48},{64,56},{72,6... | collective-permute-start | bytes 1769480 | tf_op jit(solution)/shard_map/ppermute | solution.py:22
  219.0 111.6 %collective-permute-start.12 = (bf16[384,3,256]{2,0,1:T(8,128)(2,1)}, bf16[384,3,256]{2,0,1:T(8,128)(2,1)}, u32[]{:S(2)}, u32[]{:S(2)}) collective-permute-start(bf16[384,3,256]{2,0,1:T(8,128)(2,1)} %slice.214), channel_id=1, source_target_pairs={{0,8},{8,16},{16,24},{24,32},{32,40},{40,48},{48,56},{56,64},{64,7... | collective-permute-start | bytes 1769480 | tf_op jit(solution)/shard_map/ppermute | solution.py:22
  233.6 127.7 %collective-permute-start.13 = (bf16[384,3,256]{2,0,1:T(8,128)(2,1)}, bf16[384,3,256]{2,0,1:T(8,128)(2,1)}, u32[]{:S(2)}, u32[]{:S(2)}) collective-permute-start(bf16[384,3,256]{2,0,1:T(8,128)(2,1)} %slice.214), channel_id=1, source_target_pairs={{0,16},{8,24},{16,32},{24,40},{32,48},{40,56},{48,64},{56,72},{64,... | collective-permute-start | bytes 1769480 | tf_op jit(solution)/shard_map/ppermute | solution.py:22
  256.8 116.2 %collective-permute-start.14 = (bf16[384,3,256]{2,0,1:T(8,128)(2,1)}, bf16[384,3,256]{2,0,1:T(8,128)(2,1)}, u32[]{:S(2)}, u32[]{:S(2)}) collective-permute-start(bf16[384,3,256]{2,0,1:T(8,128)(2,1)} %slice.214), channel_id=1, source_target_pairs={{0,24},{8,32},{16,40},{24,48},{32,56},{40,64},{48,72},{56,80},{64,... | collective-permute-start | bytes 1769480 | tf_op jit(solution)/shard_map/ppermute | solution.py:22
  284.5 90.4 %collective-permute-start.15 = (bf16[384,3,256]{2,0,1:T(8,128)(2,1)}, bf16[384,3,256]{2,0,1:T(8,128)(2,1)}, u32[]{:S(2)}, u32[]{:S(2)}) collective-permute-start(bf16[384,3,256]{2,0,1:T(8,128)(2,1)} %slice.214), channel_id=1, source_target_pairs={{0,32},{8,40},{16,48},{24,56},{32,64},{40,72},{48,80},{56,88},{64,... | collective-permute-start | bytes 1769480 | tf_op jit(solution)/shard_map/ppermute | solution.py:22
  328.6 48.2 %collective-permute-start.16 = (bf16[384,3,256]{2,0,1:T(8,128)(2,1)}, bf16[384,3,256]{2,0,1:T(8,128)(2,1)}, u32[]{:S(2)}, u32[]{:S(2)}) collective-permute-start(bf16[384,3,256]{2,0,1:T(8,128)(2,1)} %slice.214), channel_id=1, source_target_pairs={{0,40},{8,48},{16,56},{24,64},{32,72},{40,80},{48,88},{56,96},{64,... | collective-permute-start | bytes 1769480 | tf_op jit(solution)/shard_map/ppermute | solution.py:22
  330.6 66.9 %collective-permute-start.17 = (bf16[384,3,256]{2,0,1:T(8,128)(2,1)}, bf16[384,3,256]{2,0,1:T(8,128)(2,1)}, u32[]{:S(2)}, u32[]{:S(2)}) collective-permute-start(bf16[384,3,256]{2,0,1:T(8,128)(2,1)} %slice.214), channel_id=1, source_target_pairs={{0,48},{8,56},{16,64},{24,72},{32,80},{40,88},{48,96},{56,104},{64... | collective-permute-start | bytes 1769480 | tf_op jit(solution)/shard_map/ppermute | solution.py:22
  361.3 69.0 %collective-permute-start.18 = (bf16[384,3,256]{2,0,1:T(8,128)(2,1)}, bf16[384,3,256]{2,0,1:T(8,128)(2,1)}, u32[]{:S(2)}, u32[]{:S(2)}) collective-permute-start(bf16[384,3,256]{2,0,1:T(8,128)(2,1)} %slice.214), channel_id=1, source_target_pairs={{0,56},{8,64},{16,72},{24,80},{32,88},{40,96},{48,104},{56,112},{6... | collective-permute-start | bytes 1769480 | tf_op jit(solution)/shard_map/ppermute | solution.py:22
  373.0 208.7 %collective-permute-start.19 = (bf16[384,3,256]{2,0,1:T(8,128)(2,1)}, bf16[384,3,256]{2,0,1:T(8,128)(2,1)}, u32[]{:S(2)}, u32[]{:S(2)}) collective-permute-start(bf16[384,3,256]{2,0,1:T(8,128)(2,1)} %slice.214), channel_id=1, source_target_pairs={{0,64},{8,72},{16,80},{24,88},{32,96},{40,104},{48,112},{56,120},{... | collective-permute-start | bytes 1769480 | tf_op jit(solution)/shard_map/ppermute | solution.py:22
  374.9 212.4 %collective-permute-start.20 = (bf16[384,3,256]{2,0,1:T(8,128)(2,1)}, bf16[384,3,256]{2,0,1:T(8,128)(2,1)}, u32[]{:S(2)}, u32[]{:S(2)}) collective-permute-start(bf16[384,3,256]{2,0,1:T(8,128)(2,1)} %slice.214), channel_id=1, source_target_pairs={{0,72},{8,80},{16,88},{24,96},{32,104},{40,112},{48,120},{56,128},... | collective-permute-start | bytes 1769480 | tf_op jit(solution)/shard_map/ppermute | solution.py:22
  376.9 210.4 %collective-permute-start.21 = (bf16[384,3,256]{2,0,1:T(8,128)(2,1)}, bf16[384,3,256]{2,0,1:T(8,128)(2,1)}, u32[]{:S(2)}, u32[]{:S(2)}) collective-permute-start(bf16[384,3,256]{2,0,1:T(8,128)(2,1)} %slice.214), channel_id=1, source_target_pairs={{0,80},{8,88},{16,96},{24,104},{32,112},{40,120},{48,128},{56,136}... | collective-permute-start | bytes 1769480 | tf_op jit(solution)/shard_map/ppermute | solution.py:22
  397.4 189.9 %collective-permute-start.22 = (bf16[384,3,256]{2,0,1:T(8,128)(2,1)}, bf16[384,3,256]{2,0,1:T(8,128)(2,1)}, u32[]{:S(2)}, u32[]{:S(2)}) collective-permute-start(bf16[384,3,256]{2,0,1:T(8,128)(2,1)} %slice.214), channel_id=1, source_target_pairs={{0,88},{8,96},{16,104},{24,112},{32,120},{40,128},{48,136},{56,144... | collective-permute-start | bytes 1769480 | tf_op jit(solution)/shard_map/ppermute | solution.py:22
  430.4 157.1 %collective-permute-start.23 = (bf16[384,3,256]{2,0,1:T(8,128)(2,1)}, bf16[384,3,256]{2,0,1:T(8,128)(2,1)}, u32[]{:S(2)}, u32[]{:S(2)}) collective-permute-start(bf16[384,3,256]{2,0,1:T(8,128)(2,1)} %slice.214), channel_id=1, source_target_pairs={{0,96},{8,104},{16,112},{24,120},{32,128},{40,136},{48,144},{56,15... | collective-permute-start | bytes 1769480 | tf_op jit(solution)/shard_map/ppermute | solution.py:22
  590.7 59.6 %copy-start.3 = (f32[3072]{0:T(1024)S(1)}, f32[3072]{0:T(1024)}, u32[]{:S(2)}) copy-start(f32[3072]{0:T(1024)} %param.61) | copy-start | bytes 36868
Sparse Core Ops, SparseCore 0:
  590.8 59.3 reduce-scatter.1
